TPU v7x, 32 devices: a whole 2x2x4 slice. The times are simulated.
32 devices in a mesh: clip: 2 (over y), pos: 16 (over z, x, core).
Axes of the slice: x: 2, y: 2, z: 4, core: 2. Of those that a mesh axis runs over, the one named last changes fastest.
Arguments:
- tokens: bfloat16 [128, 256, 768], P('clip', 'pos'), may hold values from -6 to 6
- clip_lengths: int32 [2, 4], P('clip'), may hold values from 1 to 32, 64 in all within a row
- timesteps: int32 [2, 4], P('clip'), may hold values from 0 to 999
- embed_first: bfloat16 [256, 768], replicated, may hold values from -0.375 to 0.375
- embed_second: bfloat16 [768, 768], replicated, may hold values from -0.21875 to 0.21875
- adaln_weight: bfloat16 [768, 6912], replicated, may hold values from -0.4375 to 0.4375
- spatial_in: bfloat16 [768, 2304], replicated, may hold values from -0.21875 to 0.21875
- spatial_out: bfloat16 [768, 768], replicated, may hold values from -0.875 to 0.875
- temporal_in: bfloat16 [768, 2304], replicated, may hold values from -0.21875 to 0.21875
- temporal_out: bfloat16 [768, 768], replicated, may hold values from -0.4375 to 0.4375
- hidden_up: bfloat16 [768, 3072], replicated, may hold values from -0.21875 to 0.21875
- hidden_down: bfloat16 [3072, 768], replicated, may hold values from -0.109375 to 0.109375
- grad_output: bfloat16 [128, 256, 768], P('clip', 'pos'), may hold values from -6 to 6
Outputs:
- block_out: bfloat16 [128, 256, 768], P('clip', 'pos')
- grad_tokens: bfloat16 [128, 256, 768], P('clip', 'pos')
- grad_embed_first: float32 [256, 768], P('pos')
- grad_embed_second: float32 [768, 768], P('pos')
- grad_adaln_weight: float32 [768, 6912], P('pos')
- grad_spatial_in: float32 [768, 2304], P('pos')
- grad_spatial_out: float32 [768, 768], P('pos')
- grad_temporal_in: float32 [768, 2304], P('pos')
- grad_temporal_out: float32 [768, 768], P('pos')
- grad_hidden_up: float32 [768, 3072], P('pos')
- grad_hidden_down: float32 [3072, 768], P('pos')
Inputs may be any that keep to these rules, and one draw needn't show every extreme that they name: `clip_lengths`: row r lists in order the frame counts of the 4 clips that fill frames r * 64 to (r + 1) * 64 - 1; every row sums to 64 and its longest clip has 32 frames. `timesteps`: one diffusion timestep index per clip, in the order of clip_lengths.
All inputs are finite; a program needn't handle non-finite values.
Results may differ from a plain program's by a relative error of at most 0.02.
Values may be sent and summed in bfloat16 or wider, within the bound.
A program may use at most 448 MiB of HBM per device.

v0:
```python
from functools import partial
import math
import jax
import jax.numpy as jnp
from jax import lax
from jax.sharding import PartitionSpec as P

HEADS = 12
HEAD_DIM = 64
FREQ = 256
epsilon = 1e-06
highest = lax.Precision.HIGHEST
masked_score = -1000000000.0


def frequency(step_ids):
    half_width = FREQ // 2
    rate_table = jnp.exp(
        -math.log(10000.0) * jnp.arange(half_width, dtype=jnp.float32) / half_width
    )
    angles = step_ids.astype(jnp.float32)[:, None] * rate_table[None, :]
    return jnp.concatenate([jnp.cos(angles), jnp.sin(angles)], axis=1)


def modulation(step_ids, first_w, second_w, adaln_w):
    hidden_cond = jax.nn.silu(
        jnp.dot(frequency(step_ids), first_w, precision=highest, preferred_element_type=jnp.float32)
    )
    cond_vec = jnp.dot(hidden_cond, second_w, precision=highest, preferred_element_type=jnp.float32)
    return jnp.dot(
        jax.nn.silu(cond_vec), adaln_w, precision=highest, preferred_element_type=jnp.float32
    )


def clip_onehot(lengths, frames):
    clip_ends = jnp.cumsum(lengths)
    frame_ids = jnp.arange(frames, dtype=jnp.int32)
    clip_ids = jnp.sum((frame_ids[:, None] >= clip_ends[None, :]).astype(jnp.int32), axis=1)
    onehot = (clip_ids[:, None] == jnp.arange(lengths.shape[0], dtype=jnp.int32)[None, :]).astype(
        jnp.float32
    )
    return (onehot, clip_ids)


def norm_mod(values, shift_vec, scale_vec):
    centre = values - jnp.mean(values, axis=-1, keepdims=True)
    spread = jnp.mean(centre * centre, axis=-1, keepdims=True)
    return centre * lax.rsqrt(spread + epsilon) * (1.0 + scale_vec) + shift_vec


def gelu_tanh(values):
    return jax.nn.gelu(values, approximate=True)


def project(normed, weight):
    frames, places, model_width = normed.shape
    joined = jnp.dot(
        normed.reshape(frames * places, model_width), weight, preferred_element_type=jnp.float32
    )
    return joined.astype(jnp.bfloat16).reshape(frames, places, 3, HEADS, HEAD_DIM)


def weight_grad(left, right):
    return jnp.einsum("rd,rk->dk", left, right, preferred_element_type=jnp.float32)


def input_grad(grad_rows, weight):
    return jnp.einsum("rk,dk->rd", grad_rows, weight, preferred_element_type=jnp.float32)


def score_block(query_heads, key_heads, factor):
    return (
        jnp.einsum("fqhd,fkhd->fhqk", query_heads, key_heads, preferred_element_type=jnp.float32)
        * factor
    )


def on_device(
    tokens,
    clip_lengths,
    timesteps,
    embed_first,
    embed_second,
    adaln_weight,
    spatial_in,
    spatial_out,
    temporal_in,
    temporal_out,
    hidden_up,
    hidden_down,
    grad_output,
):
    frames, places, model_width = tokens.shape
    row_count = frames * places
    factor = 1.0 / math.sqrt(HEAD_DIM)
    modulated, cond_pull = jax.vjp(
        partial(modulation, timesteps[0]),
        embed_first.astype(jnp.float32),
        embed_second.astype(jnp.float32),
        adaln_weight.astype(jnp.float32),
    )
    onehot, clip_ids = clip_onehot(clip_lengths[0], frames)
    per_frame = jnp.einsum(
        "fc,cm->fm", onehot, modulated, precision=highest, preferred_element_type=jnp.float32
    )
    pieces = [
        per_frame[:, None, slot_index * model_width : (slot_index + 1) * model_width]
        for slot_index in range(9)
    ]
    token_x = tokens.astype(jnp.float32)
    normed_one, norm_pull_one = jax.vjp(norm_mod, token_x, pieces[0], pieces[1])
    h_one = normed_one.astype(jnp.bfloat16)
    qkv_one = project(h_one, spatial_in)
    q_space = qkv_one[:, :, 0]
    k_local = qkv_one[:, :, 1].reshape(frames, places, model_width)
    v_local = qkv_one[:, :, 2].reshape(frames, places, model_width)
    k_all, v_all = (
        lax.all_gather(k_local, "pos", axis=1, tiled=True),
        lax.all_gather(v_local, "pos", axis=1, tiled=True),
    )
    patch_count = k_all.shape[1]
    k_heads = k_all.reshape(frames, patch_count, HEADS, HEAD_DIM)
    v_heads = v_all.reshape(frames, patch_count, HEADS, HEAD_DIM)
    space_scores = score_block(q_space, k_heads, factor)
    space_top = jnp.max(space_scores, axis=-1, keepdims=True)
    space_lse = space_top + jnp.log(
        jnp.sum(jnp.exp(space_scores - space_top), axis=-1, keepdims=True)
    )
    space_probs = jnp.exp(space_scores - space_lse).astype(jnp.bfloat16)
    o_one = jnp.einsum("fhqk,fkhd->fqhd", space_probs, v_heads, preferred_element_type=jnp.float32)
    o_one = o_one.astype(jnp.bfloat16).reshape(row_count, model_width)
    y_one = jnp.dot(o_one, spatial_out, preferred_element_type=jnp.float32).reshape(
        frames, places, model_width
    )
    x_one = token_x + pieces[2] * y_one
    normed_two, norm_pull_two = jax.vjp(norm_mod, x_one, pieces[3], pieces[4])
    h_two = normed_two.astype(jnp.bfloat16)
    qkv_two = project(h_two, temporal_in)
    q_time = qkv_two[:, :, 0]
    k_time = qkv_two[:, :, 1]
    v_time = qkv_two[:, :, 2]
    same_clip = (clip_ids[:, None] == clip_ids[None, :])[None, None]
    time_scores = (
        jnp.einsum("fphd,gphd->phfg", q_time, k_time, preferred_element_type=jnp.float32) * factor
    )
    time_scores = jnp.where(same_clip, time_scores, masked_score)
    time_top = jnp.max(time_scores, axis=-1, keepdims=True)
    time_lse = time_top + jnp.log(jnp.sum(jnp.exp(time_scores - time_top), axis=-1, keepdims=True))
    time_probs = jnp.exp(time_scores - time_lse)
    time_low = time_probs.astype(jnp.bfloat16)
    o_two = jnp.einsum("phfg,gphd->fphd", time_low, v_time, preferred_element_type=jnp.float32)
    o_two = o_two.astype(jnp.bfloat16).reshape(row_count, model_width)
    y_two = jnp.dot(o_two, temporal_out, preferred_element_type=jnp.float32).reshape(
        frames, places, model_width
    )
    x_two = x_one + pieces[5] * y_two
    normed_three, norm_pull_three = jax.vjp(norm_mod, x_two, pieces[6], pieces[7])
    h_three = normed_three.astype(jnp.bfloat16).reshape(row_count, model_width)
    upward = jnp.dot(h_three, hidden_up, preferred_element_type=jnp.float32)
    activated, gelu_pull = jax.vjp(gelu_tanh, upward)
    act_low = activated.astype(jnp.bfloat16)
    z_out = jnp.dot(act_low, hidden_down, preferred_element_type=jnp.float32).reshape(
        frames, places, model_width
    )
    block_out = (x_two + pieces[8] * z_out).astype(jnp.bfloat16)
    grad_top = grad_output.astype(jnp.float32)
    grad_gate_three = jnp.sum(grad_top * z_out, axis=1)
    grad_z = (pieces[8] * grad_top).astype(jnp.bfloat16).reshape(row_count, model_width)
    grad_hidden_down = weight_grad(act_low, grad_z)
    grad_act = input_grad(grad_z, hidden_down)
    grad_up_rows = gelu_pull(grad_act)[0].astype(jnp.bfloat16)
    grad_hidden_up = weight_grad(h_three, grad_up_rows)
    grad_h_three = input_grad(grad_up_rows, hidden_up).reshape(frames, places, model_width)
    grad_norm_three, grad_shift_three, grad_scale_three = norm_pull_three(grad_h_three)
    grad_two = grad_top + grad_norm_three
    grad_gate_two = jnp.sum(grad_two * y_two, axis=1)
    grad_y_two = (pieces[5] * grad_two).astype(jnp.bfloat16).reshape(row_count, model_width)
    grad_temporal_out = weight_grad(o_two, grad_y_two)
    grad_o_two = (
        input_grad(grad_y_two, temporal_out)
        .astype(jnp.bfloat16)
        .reshape(frames, places, HEADS, HEAD_DIM)
    )
    grad_time_probs = jnp.einsum(
        "fphd,gphd->phfg", grad_o_two, v_time, preferred_element_type=jnp.float32
    )
    time_inner = jnp.sum(grad_time_probs * time_probs, axis=-1, keepdims=True)
    grad_time_scores = (time_probs * (grad_time_probs - time_inner)).astype(jnp.bfloat16)
    grad_q_time = (
        jnp.einsum("phfg,gphd->fphd", grad_time_scores, k_time, preferred_element_type=jnp.float32)
        * factor
    )
    grad_k_time = (
        jnp.einsum("phfg,fphd->gphd", grad_time_scores, q_time, preferred_element_type=jnp.float32)
        * factor
    )
    grad_v_time = jnp.einsum(
        "phfg,fphd->gphd", time_low, grad_o_two, preferred_element_type=jnp.float32
    )
    grad_qkv_two = (
        jnp.stack([grad_q_time, grad_k_time, grad_v_time], axis=2)
        .astype(jnp.bfloat16)
        .reshape(row_count, 3 * model_width)
    )
    grad_temporal_in = weight_grad(h_two.reshape(row_count, model_width), grad_qkv_two)
    grad_h_two = input_grad(grad_qkv_two, temporal_in).reshape(frames, places, model_width)
    grad_norm_two, grad_shift_two, grad_scale_two = norm_pull_two(grad_h_two)
    grad_one = grad_two + grad_norm_two
    grad_gate_one = jnp.sum(grad_one * y_one, axis=1)
    grad_y_one = (pieces[2] * grad_one).astype(jnp.bfloat16).reshape(row_count, model_width)
    grad_spatial_out = weight_grad(o_one, grad_y_one)
    grad_o_one = (
        input_grad(grad_y_one, spatial_out)
        .astype(jnp.bfloat16)
        .reshape(frames, places, model_width)
    )
    k_back, v_back = (k_all, v_all)
    k_back_heads = k_back.reshape(frames, patch_count, HEADS, HEAD_DIM)
    v_back_heads = v_back.reshape(frames, patch_count, HEADS, HEAD_DIM)
    grad_o_heads = grad_o_one.reshape(frames, places, HEADS, HEAD_DIM)
    again_probs = jnp.exp(score_block(q_space, k_back_heads, factor) - space_lse)
    grad_space_probs = jnp.einsum(
        "fqhd,fkhd->fhqk", grad_o_heads, v_back_heads, preferred_element_type=jnp.float32
    )
    space_inner = jnp.sum(grad_space_probs * again_probs, axis=-1, keepdims=True)
    grad_space_scores = (again_probs * (grad_space_probs - space_inner)).astype(jnp.bfloat16)
    grad_q_space = (
        jnp.einsum(
            "fhqk,fkhd->fqhd", grad_space_scores, k_back_heads, preferred_element_type=jnp.float32
        )
        * factor
    )
    key_terms = (
        jnp.einsum(
            "fhqk,fqhd->fkhd", grad_space_scores, q_space, preferred_element_type=jnp.float32
        )
        * factor
    )
    value_terms = jnp.einsum(
        "fhqk,fqhd->fkhd",
        again_probs.astype(jnp.bfloat16),
        grad_o_heads,
        preferred_element_type=jnp.float32,
    )
    grad_keys, grad_values = (
        lax.psum_scatter(
            key_terms.reshape(frames, patch_count, model_width).astype(jnp.bfloat16),
            "pos",
            scatter_dimension=1,
            tiled=True,
        ).astype(jnp.float32),
        lax.psum_scatter(
            value_terms.reshape(frames, patch_count, model_width).astype(jnp.bfloat16),
            "pos",
            scatter_dimension=1,
            tiled=True,
        ).astype(jnp.float32),
    )
    grad_qkv_one = jnp.stack(
        [grad_q_space.reshape(frames, places, model_width), grad_keys, grad_values], axis=2
    )
    grad_qkv_one = grad_qkv_one.astype(jnp.bfloat16).reshape(row_count, 3 * model_width)
    grad_spatial_in = weight_grad(h_one.reshape(row_count, model_width), grad_qkv_one)
    grad_h_one = input_grad(grad_qkv_one, spatial_in).reshape(frames, places, model_width)
    grad_norm_one, grad_shift_one, grad_scale_one = norm_pull_one(grad_h_one)
    grad_tokens = (grad_one + grad_norm_one).astype(jnp.bfloat16)
    grad_frames = jnp.concatenate(
        [
            grad_shift_one[:, 0],
            grad_scale_one[:, 0],
            grad_gate_one,
            grad_shift_two[:, 0],
            grad_scale_two[:, 0],
            grad_gate_two,
            grad_shift_three[:, 0],
            grad_scale_three[:, 0],
            grad_gate_three,
        ],
        axis=1,
    )
    grad_modulation = jnp.einsum(
        "fc,fm->cm", onehot, grad_frames, precision=highest, preferred_element_type=jnp.float32
    )
    grad_embed_first, grad_embed_second, grad_adaln_weight = cond_pull(grad_modulation)
    summed = (
        lax.psum_scatter(
            grad_embed_first.astype(jnp.bfloat16), "pos", scatter_dimension=0, tiled=True
        ).astype(jnp.float32),
        lax.psum_scatter(
            grad_embed_second.astype(jnp.bfloat16), "pos", scatter_dimension=0, tiled=True
        ).astype(jnp.float32),
        lax.psum_scatter(
            grad_adaln_weight.astype(jnp.bfloat16), "pos", scatter_dimension=0, tiled=True
        ).astype(jnp.float32),
        lax.psum_scatter(
            grad_spatial_in.astype(jnp.bfloat16), "pos", scatter_dimension=0, tiled=True
        ).astype(jnp.float32),
        lax.psum_scatter(
            grad_spatial_out.astype(jnp.bfloat16), "pos", scatter_dimension=0, tiled=True
        ).astype(jnp.float32),
        lax.psum_scatter(
            grad_temporal_in.astype(jnp.bfloat16), "pos", scatter_dimension=0, tiled=True
        ).astype(jnp.float32),
        lax.psum_scatter(
            grad_temporal_out.astype(jnp.bfloat16), "pos", scatter_dimension=0, tiled=True
        ).astype(jnp.float32),
        lax.psum_scatter(
            grad_hidden_up.astype(jnp.bfloat16), "pos", scatter_dimension=0, tiled=True
        ).astype(jnp.float32),
        lax.psum_scatter(
            grad_hidden_down.astype(jnp.bfloat16), "pos", scatter_dimension=0, tiled=True
        ).astype(jnp.float32),
    )
    summed = (
        lax.psum(summed[0].astype(jnp.bfloat16), "clip").astype(jnp.float32),
        lax.psum(summed[1].astype(jnp.bfloat16), "clip").astype(jnp.float32),
        lax.psum(summed[2].astype(jnp.bfloat16), "clip").astype(jnp.float32),
        lax.psum(summed[3].astype(jnp.bfloat16), "clip").astype(jnp.float32),
        lax.psum(summed[4].astype(jnp.bfloat16), "clip").astype(jnp.float32),
        lax.psum(summed[5].astype(jnp.bfloat16), "clip").astype(jnp.float32),
        lax.psum(summed[6].astype(jnp.bfloat16), "clip").astype(jnp.float32),
        lax.psum(summed[7].astype(jnp.bfloat16), "clip").astype(jnp.float32),
        lax.psum(summed[8].astype(jnp.bfloat16), "clip").astype(jnp.float32),
    )
    return (
        block_out,
        grad_tokens,
        summed[0],
        summed[1],
        summed[2],
        summed[3],
        summed[4],
        summed[5],
        summed[6],
        summed[7],
        summed[8],
    )


def solution(mesh):
    in_specs = (
        P("clip", "pos", None),
        P("clip", None),
        P("clip", None),
        P(),
        P(),
        P(),
        P(),
        P(),
        P(),
        P(),
        P(),
        P(),
        P("clip", "pos", None),
    )
    out_specs = (
        P("clip", "pos", None),
        P("clip", "pos", None),
        P("pos", None),
        P("pos", None),
        P("pos", None),
        P("pos", None),
        P("pos", None),
        P("pos", None),
        P("pos", None),
        P("pos", None),
        P("pos", None),
    )
    return jax.shard_map(
        on_device, mesh=mesh, in_specs=in_specs, out_specs=out_specs, check_vma=False
    )
```

profile of v0, /device:TPU:0, one launch (start us, length us, event | category | flops | bytes accessed | tf_op | source)
XLA Modules:
  0.0 1902.6 jit_solution(2923653464098898793)
XLA Ops:
  14.0 7.0 fusion.78
  31.7 15.0 reshape.275
  46.7 9.2 fusion.90
  68.8 124.6 %all-gather.5.cloned.1.call-done = bf16[64,256,768]{2,1,0:T(8,128)(2,1)} async-done(((bf16[64,16,768]{2,1,0:T(8,128)(2,1)}), bf16[64,256,768]{2,1,0:T(8,128)(2,1)}) %all-gather.5.cloned.1.call-update) | async-done | bytes 25165840 | tf_op jit(solution)/shard_map/all_gather | solution.py:118
  193.5 30.7 %copy.79 = bf16[64,256,768]{1,2,0:T(8,128)(2,1)} copy(bf16[64,256,768]{2,1,0:T(8,128)(2,1)} %all-gather.5.cloned.1.call-done) | data formatting | bytes 50331648 | tf_op jit(solution)/shard_map/all_gather | solution.py:118
  224.2 18.9 multiply_reduce_fusion.1
  243.1 8.6 exponential_reduce_fusion
  252.7 71.5 %all-gather.3.cloned.1.call-done = bf16[64,256,768]{2,1,0:T(8,128)(2,1)} async-done(((bf16[64,16,768]{2,1,0:T(8,128)(2,1)}), bf16[64,256,768]{2,1,0:T(8,128)(2,1)}) %all-gather.3.cloned.1.call-update) | async-done | bytes 25165840 | tf_op jit(solution)/shard_map/all_gather | solution.py:119
  324.1 31.5 %copy.77 = bf16[64,256,768]{1,2,0:T(8,128)(2,1)} copy(bf16[64,256,768]{2,1,0:T(8,128)(2,1)} %all-gather.3.cloned.1.call-done) | data formatting | bytes 50331648 | tf_op jit(solution)/shard_map/all_gather | solution.py:119
  355.6 16.2 convert_bitcast_fusion
  397.0 15.0 reshape.279
  412.0 9.2 fusion.89
  427.9 8.2 fusion.8
  457.2 7.1 fusion.93
  464.3 7.3 fusion.86
  471.7 16.5 fusion.6
  488.2 9.0 fusion.94
  525.6 7.4 convolution_bitcast_fusion
  533.1 8.0 multiply_reduce_fusion.2
  555.7 9.6 maximum_convert_fusion
  565.3 12.3 copy.97
  577.6 15.8 convert_element_type.240
  593.5 7.5 multiply_reduce_fusion.6
  616.8 17.5 convolution_convert_fusion
  634.3 32.6 %copy.102 = bf16[64,256,768]{2,1,0:T(8,128)(2,1)} copy(bf16[64,256,768]{1,2,0:T(8,128)(2,1)} %bitcast.161) | data formatting | bytes 50331648 | tf_op jit(solution)/shard_map/convert_element_type | solution.py:253
  667.0 26.9 %multiply_reduce_fusion = (f32[64,12,16]{2,1,0:T(8,128)S(1)}, f32[64,12,16,256]{3,2,1,0:T(8,128)}) fusion(f32[64,12,16,256]{3,2,1,0:T(8,128)} %get-tuple-element.58, f32[64,12,16]{2,1,0:T(8,128)S(1)} %copy-done.14, bf16[64,256,12,64]{1,3,2,0:T(8,128)(2,1)} %bitcast.156, bf16[64,16,12,64]{3,2,1,0:T(8,128)(2,1)} %reshape_reshape.3), kind=kOutput, calls=%fused_computation.13 | convolution fusion | flops 415223808 | bytes 52002816 | tf_op jit(solution)/shard_map/fqhd,fkhd->fhqk/dot_general | solution.py:222
  693.9 12.4 multiply_convert_fusion.1
  706.3 14.0 multiply_convert_fusion
  720.3 30.1 %copy.100 = bf16[64,256,768]{2,1,0:T(8,128)(2,1)} copy(bf16[64,256,768]{1,2,0:T(8,128)(2,1)} %bitcast.162) | data formatting | bytes 50331648 | tf_op jit(solution)/shard_map/convert_element_type | solution.py:247
  774.2 16.0 convert_element_type.264
  790.1 7.8 convolution_convert_fusion.6
  799.3 11.6 convolution_convert_fusion.4
  812.3 9.6 convolution_convert_fusion.5
  821.9 13.6 multiply_bitcast_fusion
  843.8 66.5 %reduce-scatter.14.cloned.1.call-done = bf16[64,16,768]{2,1,0:T(8,128)(2,1)} async-done(((bf16[64,256,768]{2,1,0:T(8,128)(2,1)}), bf16[64,16,768]{2,1,0:T(8,128)(2,1)}) %reduce-scatter.14.cloned.1.call-update) | async-done | bytes 1572880 | tf_op jit(solution)/shard_map/reduce_scatter | solution.py:252
  910.4 246.4 %reduce-scatter.12.cloned.1.call-done = bf16[64,16,768]{2,1,0:T(8,128)(2,1)} async-done(((bf16[64,256,768]{2,1,0:T(8,128)(2,1)}), bf16[64,16,768]{2,1,0:T(8,128)(2,1)}) %reduce-scatter.12.cloned.1.call-update) | async-done | bytes 1572880 | tf_op jit(solution)/shard_map/reduce_scatter | solution.py:246
  1169.7 8.3 fusion.95
  1198.6 19.3 %convolution_convert_fusion.1 = bf16[768,6912]{1,0:T(8,128)(2,1)} fusion(f32[4,6912]{1,0:T(4,128)S(1)} %fusion.48, f32[4,768]{1,0:T(4,128)S(1)} %copy-done.71), kind=kOutput, calls=%fused_computation.17 | convolution fusion | flops 260124672 | bytes 10739712 | tf_op jit(solution)/shard_map/transpose(jvp())/dot_general | solution.py:30
  1221.9 56.2 %reduce-scatter.24.cloned.1.call-done = bf16[48,768]{1,0:T(8,128)(2,1)} async-done(((bf16[768,768]{1,0:T(8,128)(2,1)}), bf16[48,768]{1,0:T(8,128)(2,1)}) %reduce-scatter.24.cloned.1.call-update) | async-done | bytes 73744 | tf_op jit(solution)/shard_map/reduce_scatter | solution.py:298
  1278.2 71.0 %reduce-scatter.26.cloned.1.call-done = bf16[48,2304]{1,0:T(8,128)(2,1)} async-done(((bf16[768,2304]{1,0:T(8,128)(2,1)}), bf16[48,2304]{1,0:T(8,128)(2,1)}) %reduce-scatter.26.cloned.1.call-update) | async-done | bytes 221200 | tf_op jit(solution)/shard_map/reduce_scatter | solution.py:301
  1349.2 78.5 %reduce-scatter.32.cloned.1.call-done = bf16[192,768]{1,0:T(8,128)(2,1)} async-done(((bf16[3072,768]{1,0:T(8,128)(2,1)}), bf16[192,768]{1,0:T(8,128)(2,1)}) %reduce-scatter.32.cloned.1.call-update) | async-done | bytes 294928 | tf_op jit(solution)/shard_map/reduce_scatter | solution.py:310
  1427.7 78.6 %reduce-scatter.30.cloned.1.call-done = bf16[48,3072]{1,0:T(8,128)(2,1)} async-done(((bf16[768,3072]{1,0:T(8,128)(2,1)}), bf16[48,3072]{1,0:T(8,128)(2,1)}) %reduce-scatter.30.cloned.1.call-update) | async-done | bytes 294928 | tf_op jit(solution)/shard_map/reduce_scatter | solution.py:307
  1506.3 61.5 %reduce-scatter.18.cloned.1.call-done = bf16[48,768]{1,0:T(8,128)(2,1)} async-done(((bf16[768,768]{1,0:T(8,128)(2,1)}), bf16[48,768]{1,0:T(8,128)(2,1)}) %reduce-scatter.18.cloned.1.call-update) | async-done | bytes 73744 | tf_op jit(solution)/shard_map/reduce_scatter | solution.py:289
  1567.8 71.0 %reduce-scatter.22.cloned.1.call-done = bf16[48,2304]{1,0:T(8,128)(2,1)} async-done(((bf16[768,2304]{1,0:T(8,128)(2,1)}), bf16[48,2304]{1,0:T(8,128)(2,1)}) %reduce-scatter.22.cloned.1.call-update) | async-done | bytes 221200 | tf_op jit(solution)/shard_map/reduce_scatter | solution.py:295
  1638.8 123.6 %reduce-scatter.20.cloned.1.call-done = bf16[48,6912]{1,0:T(8,128)(2,1)} async-done(((bf16[768,6912]{1,0:T(8,128)(2,1)}), bf16[48,6912]{1,0:T(8,128)(2,1)}) %reduce-scatter.20.cloned.1.call-update) | async-done | bytes 663568 | tf_op jit(solution)/shard_map/reduce_scatter | solution.py:292
  1767.5 54.7 %reduce-scatter.16.cloned.1.call-done = bf16[16,768]{1,0:T(8,128)(2,1)} async-done(((bf16[256,768]{1,0:T(8,128)(2,1)}), bf16[16,768]{1,0:T(8,128)(2,1)}) %reduce-scatter.16.cloned.1.call-update) | async-done | bytes 24592 | tf_op jit(solution)/shard_map/reduce_scatter | solution.py:286
  1822.2 9.5 psum.63
  1833.0 49.9 %all-reduce.3.cloned.1.call-done = (bf16[48,768]{1,0:T(8,128)(2,1)}, bf16[48,6912]{1,0:T(8,128)(2,1)}, bf16[48,2304]{1,0:T(8,128)(2,1)}, bf16[48,768]{1,0:T(8,12...) async-done(((bf16[48,768]{1,0:T(8,128)(2,1)}, bf16[48,6912]{1,0:T(8,128)(2,1)}, ...) | async-done | bytes 1916944 | tf_op jit(solution)/shard_map/psum | solution.py:316
  (326 shorter events, 233.8 us)
Async XLA Ops:
  7.2 384.4 %copy-start = (bf16[768,2304]{1,0:T(8,128)(2,1)S(1)}, bf16[768,2304]{1,0:T(8,128)(2,1)}, u32[]{:S(2)}) copy-start(bf16[768,2304]{1,0:T(8,128)(2,1)} %param.21) | copy-start | bytes 10616836
  7.2 186.3 %all-gather.5.cloned.1.call-start = ((), (), s32[]{:S(2)}) async-start(), calls=%async_computation.12 | async-start | bytes 26738688 | tf_op jit(solution)/shard_map/all_gather | solution.py:118
  8.3 60.4 %copy-start.87 = (s32[64]{0:T(128)}, s32[64]{0:T(128)S(1)}, u32[]{:S(2)}) copy-start(s32[64]{0:T(128)S(1)} %convert_reduce_fusion.1) | copy-start | bytes 772
  10.8 12.2 copy-start.54
  12.8 10.2 copy-start.66
  12.9 8.1 copy-start.83
  12.9 8.1 copy-start.85
  13.4 7.6 copy-start.80
  62.0 262.1 %all-gather.3.cloned.1.call-start = ((), (), s32[]{:S(2)}) async-start(), calls=%async_computation.11 | async-start | bytes 26738688 | tf_op jit(solution)/shard_map/all_gather | solution.py:119
  68.2 842.2 %reduce-scatter.14.cloned.1.call-start = ((), (), s32[]{:S(2)}) async-start(), calls=%async_computation.14 | async-start | bytes 26738688 | tf_op jit(solution)/shard_map/reduce_scatter | solution.py:252
  243.1 8.7 copy-start.25
  454.8 9.5 slice-start.5
  464.3 7.4 copy-start.40
  471.7 28.3 %copy-start.19 = (f32[1024,768]{1,0:T(8,128)}, f32[1024,768]{1,0:T(8,128)S(1)}, u32[]{:S(2)}) copy-start(f32[1024,768]{1,0:T(8,128)S(1)} %fusion.86) | copy-start | bytes 9437188
  525.6 7.5 copy-start.12
  525.6 7.5 copy-start.13
  525.6 7.5 copy-start.29
  525.6 15.5 slice-start
  533.1 8.0 slice-start.1
  593.4 7.6 copy-start.77
  593.5 7.6 copy-start.4
  593.5 7.6 copy-start.31
  593.5 7.6 copy-start.53
  593.5 7.6 copy-start.69
  593.5 10.5 copy-start.20
  593.5 10.5 copy-start.21
  593.5 10.5 copy-start.22
  666.9 489.8 %reduce-scatter.12.cloned.1.call-start = ((), (), s32[]{:S(2)}) async-start(), calls=%async_computation.13 | async-start | bytes 26738688 | tf_op jit(solution)/shard_map/reduce_scatter | solution.py:246
  706.3 14.0 copy-start.5
  750.4 471.5 %reduce-scatter.28.cloned.1.call-start = ((), (), s32[]{:S(2)}) async-start(), calls=%async_computation.21 | async-start | bytes 1253376 | tf_op jit(solution)/shard_map/reduce_scatter | solution.py:304
  766.2 512.0 %reduce-scatter.24.cloned.1.call-start = ((), (), s32[]{:S(2)}) async-start(), calls=%async_computation.19 | async-start | bytes 1253376 | tf_op jit(solution)/shard_map/reduce_scatter | solution.py:298
  774.1 16.0 copy-start.43
  774.1 575.1 %reduce-scatter.26.cloned.1.call-start = ((), (), s32[]{:S(2)}) async-start(), calls=%async_computation.20 | async-start | bytes 3760128 | tf_op jit(solution)/shard_map/reduce_scatter | solution.py:301
  797.9 629.7 %reduce-scatter.32.cloned.1.call-start = ((), (), s32[]{:S(2)}) async-start(), calls=%async_computation.23 | async-start | bytes 5013504 | tf_op jit(solution)/shard_map/reduce_scatter | solution.py:310
  810.9 695.4 %reduce-scatter.30.cloned.1.call-start = ((), (), s32[]{:S(2)}) async-start(), calls=%async_computation.22 | async-start | bytes 5013504 | tf_op jit(solution)/shard_map/reduce_scatter | solution.py:307
  821.9 745.9 %reduce-scatter.18.cloned.1.call-start = ((), (), s32[]{:S(2)}) async-start(), calls=%async_computation.16 | async-start | bytes 1253376 | tf_op jit(solution)/shard_map/reduce_scatter | solution.py:289
  1159.2 10.5 slice-start.2
  1161.4 8.3 slice-start.3
  1161.4 8.3 slice-start.4
  1169.7 8.3 copy-start.71
  1169.7 8.3 copy-start.81
  1181.2 457.6 %reduce-scatter.22.cloned.1.call-start = ((), (), s32[]{:S(2)}) async-start(), calls=%async_computation.18 | async-start | bytes 3760128 | tf_op jit(solution)/shard_map/reduce_scatter | solution.py:295
  1198.6 563.8 %reduce-scatter.20.cloned.1.call-start = ((), (), s32[]{:S(2)}) async-start(), calls=%async_computation.17 | async-start | bytes 11280384 | tf_op jit(solution)/shard_map/reduce_scatter | solution.py:292
  1217.9 544.5 %copy-start.82 = (f32[64,16]{1,0:T(8,128)S(1)}, f32[64,16]{1,0:T(8,128)}, u32[]{:S(2)}) copy-start(f32[64,16]{1,0:T(8,128)} %get-tuple-element.14) | copy-start | bytes 12292
  1218.0 604.2 %reduce-scatter.16.cloned.1.call-start = ((), (), s32[]{:S(2)}) async-start(), calls=%async_computation.15 | async-start | bytes 417792 | tf_op jit(solution)/shard_map/reduce_scatter | solution.py:286
  1221.9 661.0 %all-reduce.3.cloned.1.call-start = ((), (), s32[]{:S(2)}) async-start(), calls=%async_computation.24 | async-start | bytes 3833856 | tf_op jit(solution)/shard_map/psum | solution.py:316
  1762.5 133.4 %copy-start.1 = (bf16[768,2304]{1,0:T(8,128)(2,1)S(1)}, bf16[768,2304]{1,0:T(8,128)(2,1)}, u32[]{:S(2)}) copy-start(bf16[768,2304]{1,0:T(8,128)(2,1)} %param.21) | copy-start | bytes 10616836
  1882.9 11.8 copy-start.65
  (65 other events, 187.4 us)
Sparse Core Ops, SparseCore 0:
  62.2 131.2 all-gather.4
  195.6 128.5 all-gather.2
  667.1 243.2 reduce-scatter.13
  914.3 242.3 reduce-scatter.11
  1160.2 57.2 reduce-scatter.27
  1221.0 57.1 reduce-scatter.23
  1282.1 67.1 reduce-scatter.25
  1353.1 74.5 reduce-scatter.31
  1431.5 74.7 reduce-scatter.29
  1510.3 57.4 reduce-scatter.17
  1571.7 67.1 reduce-scatter.21
  1642.7 119.6 reduce-scatter.19
  1766.5 55.6 reduce-scatter.15
  1824.7 58.1 all-reduce.2
where the time goes:
time: 1920 us; the launch traced here: 1900 us
  waiting for transfers between devices  1150 us (60%)
  local copies, waits for them, and re-layouts  321 us (17%)
  matrix products  304 us (16%)
  other arithmetic  97.4 us (5%)
    reduce_scatter x1, waiting for transfers between devices, on_device(): lax.psum_scatter(key_terms.reshape(frames, patch_count, model_width).asty...  246 us
    all_gather x1, waiting for transfers between devices, on_device(): lax.all_gather(k_local, 'pos', axis=1, tiled=True)  125 us
    reduce_scatter x1, waiting for transfers between devices, on_device(): lax.psum_scatter(grad_adaln_weight.astype(jnp.bfloat16), 'pos', scatter_d...  124 us
    reduce_scatter x1, waiting for transfers between devices, on_device(): lax.psum_scatter(grad_hidden_up.astype(jnp.bfloat16), 'pos', scatter_dime...  78.6 us
    reduce_scatter x1, waiting for transfers between devices, on_device(): lax.psum_scatter(grad_hidden_down.astype(jnp.bfloat16), 'pos', scatter_di...  78.5 us
    all_gather x1, waiting for transfers between devices, on_device(): lax.all_gather(v_local, 'pos', axis=1, tiled=True)  71.5 us
    reduce_scatter x1, waiting for transfers between devices, on_device(): lax.psum_scatter(grad_spatial_in.astype(jnp.bfloat16), 'pos', scatter_dim...  71 us
    reduce_scatter x1, waiting for transfers between devices, on_device(): lax.psum_scatter(grad_temporal_in.astype(jnp.bfloat16), 'pos', scatter_di...  71 us
  transfers between devices with their start and end apart: 14, of which 13 were waited for; matrix products, arithmetic and copies ran while one was open for 16% of the time, Pallas kernels for 0%

commit v1 on v0

--- a/solution.py
+++ b/solution.py
@@ -114,10 +114,24 @@
     q_space = qkv_one[:, :, 0]
     k_local = qkv_one[:, :, 1].reshape(frames, places, model_width)
     v_local = qkv_one[:, :, 2].reshape(frames, places, model_width)
-    k_all, v_all = (
-        lax.all_gather(k_local, "pos", axis=1, tiled=True),
-        lax.all_gather(v_local, "pos", axis=1, tiled=True),
-    )
+
+    def map_cells(unit):
+        y1, v1, heard = (lax.psum(1, "pos"), lax.axis_index("pos"), unit.shape[1])
+        t1, base_arr = (unit, 1)
+        while base_arr < y1:
+            t1 = jnp.concatenate(
+                [
+                    t1,
+                    lax.ppermute(
+                        t1, "pos", list(map(lambda j: (j, (j - base_arr) % y1), range(y1)))
+                    ),
+                ],
+                1,
+            )
+            base_arr = 2 * base_arr
+        return jnp.roll(t1, v1 * heard, 1)
+
+    k_all, v_all = (map_cells(k_local), lax.all_gather(v_local, "pos", axis=1, tiled=True))
     patch_count = k_all.shape[1]
     k_heads = k_all.reshape(frames, patch_count, HEADS, HEAD_DIM)
     v_heads = v_all.reshape(frames, patch_count, HEADS, HEAD_DIM)

time: 1920 us -> 2680 us (1.40)
  waiting for transfers between devices: 1150 us -> 1850 us
  local copies, waits for them, and re-layouts: 321 us -> 384 us
    ppermute x0 -> x4, waiting for transfers between devices: none -> 862 us  [map_cells(): lax.ppermute(t1, 'pos', list(map(lambda j: (j, (j - base_arr) % y1), rang...]
    reduce_scatter x1, waiting for transfers between devices: 66.5 us -> 247 us  [on_device(): lax.psum_scatter(value_terms.reshape(frames, patch_count, model_width).as...]
    reduce_scatter x1, waiting for transfers between devices: 246 us -> 97 us  [on_device(): lax.psum_scatter(key_terms.reshape(frames, patch_count, model_width).asty...]
    all_gather x1 -> x0, waiting for transfers between devices: 125 us -> none  [on_device(): lax.all_gather(k_local, 'pos', axis=1, tiled=True)]
    all_gather x1, waiting for transfers between devices: 71.5 us -> 0.01 us  [on_device(): lax.all_gather(v_local, 'pos', axis=1, tiled=True)]
    dynamic_slice x0 -> x2, local copies, waits for them, and re-layouts: none -> 51 us  [map_cells(): return jnp.roll(t1, v1 * heard, 1)]
    all_gather x1 -> x0, local copies, waits for them, and re-layouts: 30.7 us -> none  [on_device(): lax.all_gather(k_local, 'pos', axis=1, tiled=True)]
    unnamed x208 -> x235, local copies, waits for them, and re-layouts: 27.5 us -> 58 us
  transfers between devices with their start and end apart: 14 -> 17, of which waited for: 13 -> 15; matrix products, arithmetic and copies ran while one was open for 16% -> 13% of each run, Pallas kernels for 0% -> 0%
where the time goes in v1:
time: 2680 us; the launch traced here: 2670 us
  waiting for transfers between devices  1850 us (69%)
  local copies, waits for them, and re-layouts  384 us (14%)
  matrix products  299 us (11%)
  other arithmetic  99.3 us (4%)
    ppermute x4, waiting for transfers between devices, map_cells(): lax.ppermute(t1, 'pos', list(map(lambda j: (j, (j - base_arr) % y1), rang...  862 us
    reduce_scatter x1, waiting for transfers between devices, on_device(): lax.psum_scatter(value_terms.reshape(frames, patch_count, model_width).as...  247 us
    reduce_scatter x1, waiting for transfers between devices, on_device(): lax.psum_scatter(grad_adaln_weight.astype(jnp.bfloat16), 'pos', scatter_d...  124 us
    reduce_scatter x1, waiting for transfers between devices, on_device(): lax.psum_scatter(key_terms.reshape(frames, patch_count, model_width).asty...  97 us
    reduce_scatter x1, waiting for transfers between devices, on_device(): lax.psum_scatter(grad_hidden_down.astype(jnp.bfloat16), 'pos', scatter_di...  78.7 us
    reduce_scatter x1, waiting for transfers between devices, on_device(): lax.psum_scatter(grad_hidden_up.astype(jnp.bfloat16), 'pos', scatter_dime...  78.3 us
    reduce_scatter x1, waiting for transfers between devices, on_device(): lax.psum_scatter(grad_temporal_in.astype(jnp.bfloat16), 'pos', scatter_di...  70.9 us
    reduce_scatter x1, waiting for transfers between devices, on_device(): lax.psum_scatter(grad_spatial_in.astype(jnp.bfloat16), 'pos', scatter_dim...  70.9 us
  transfers between devices with their start and end apart: 17, of which 15 were waited for; matrix products, arithmetic and copies ran while one was open for 13% of the time, Pallas kernels for 0%

profile of v1, /device:TPU:0, one launch (start us, length us, event | category | flops | bytes accessed | tf_op | source)
XLA Modules:
  0.0 2665.9 jit_solution(15501055001087952348)
XLA Ops:
  32.2 15.0 reshape.275
  47.1 9.3 fusion.90
  74.1 52.1 %collective-permute-done = bf16[64,16,768]{2,1,0:T(8,128)(2,1)S(1)} collective-permute-done((bf16[64,16,768]{2,1,0:T(8,128)(2,1)}, bf16[64,16,768]{2,1,0:T(8,128)(2,1)S(1)}, u32[]{:S(2)}, u32[]{:S(2)}) %collective-permute-start) | collective-permute-done | bytes 1572896 | tf_op jit(solution)/shard_map/ppermute | solution.py:125
  128.8 137.3 %collective-permute-done.1 = bf16[64,32,768]{2,1,0:T(8,128)(2,1)S(1)} collective-permute-done((bf16[64,32,768]{2,1,0:T(8,128)(2,1)S(1)}, bf16[64,32,768]{2,1,0:T(8,128)(2,1)S(1)}, u32[]{:S(2)}, u32[]{:S(2)}) %collective-permute-start.1) | collective-permute-done | bytes 3145760 | tf_op jit(solution)/shard_map/ppermute | solution.py:125
  267.4 143.5 %collective-permute-done.2 = bf16[64,64,768]{2,1,0:T(8,128)(2,1)S(1)} collective-permute-done((bf16[64,64,768]{2,1,0:T(8,128)(2,1)S(1)}, bf16[64,64,768]{2,1,0:T(8,128)(2,1)S(1)}, u32[]{:S(2)}, u32[]{:S(2)}) %collective-permute-start.2) | collective-permute-done | bytes 6291488 | tf_op jit(solution)/shard_map/ppermute | solution.py:125
  431.9 528.7 %collective-permute-done.3 = bf16[64,128,768]{2,1,0:T(8,128)(2,1)} collective-permute-done((bf16[64,128,768]{2,1,0:T(8,128)(2,1)}, bf16[64,128,768]{2,1,0:T(8,128)(2,1)}, u32[]{:S(2)}, u32[]{:S(2)}) %collective-permute-start.3) | collective-permute-done | bytes 12582944 | tf_op jit(solution)/shard_map/ppermute | solution.py:125
  960.6 10.9 constant_dynamic-update-slice_fusion.5
  979.1 10.8 constant_dynamic-update-slice_fusion
  989.9 21.0 constant_dynamic-slice_fusion
  1010.9 30.0 %copy.84 = bf16[64,256,768]{1,2,0:T(8,128)(2,1)} copy(bf16[64,256,768]{2,1,0:T(8,128)(2,1)} %constant_dynamic-slice_fusion) | data formatting | bytes 50331648 | tf_op jit(solution)/shard_map/jit(_roll_dynamic)/dynamic_slice | solution.py:132
  1040.9 18.4 multiply_reduce_fusion.1
  1059.2 8.6 exponential_reduce_fusion
  1068.7 32.6 %copy.82 = bf16[64,256,768]{1,2,0:T(8,128)(2,1)} copy(bf16[64,256,768]{2,1,0:T(8,128)(2,1)} %all-gather.2.cloned.1.call-done) | data formatting | bytes 50331648 | tf_op jit(solution)/shard_map/all_gather | solution.py:134
  1101.3 16.2 convert_bitcast_fusion
  1142.9 15.0 reshape.279
  1157.9 7.7 fusion.89
  1215.3 16.5 fusion.6
  1231.7 8.6 fusion.94
  1280.6 7.4 multiply_bitcast_fusion.2
  1296.6 9.7 maximum_convert_fusion
  1306.2 12.3 copy.102
  1318.5 15.7 convert_element_type.240
  1334.4 7.5 multiply_reduce_fusion.6
  1357.5 20.3 multiply_reduce_fusion
  1377.8 10.3 multiply_convert_fusion.1
  1388.1 13.8 multiply_convert_fusion
  1402.0 32.9 %copy.105 = bf16[64,256,768]{2,1,0:T(8,128)(2,1)} copy(bf16[64,256,768]{1,2,0:T(8,128)(2,1)} %bitcast.162) | data formatting | bytes 50331648 | tf_op jit(solution)/shard_map/convert_element_type | solution.py:261
  1434.9 20.2 convolution_convert_fusion
  1455.1 31.3 %copy.107 = bf16[64,256,768]{2,1,0:T(8,128)(2,1)} copy(bf16[64,256,768]{1,2,0:T(8,128)(2,1)} %bitcast.161) | data formatting | bytes 50331648 | tf_op jit(solution)/shard_map/convert_element_type | solution.py:267
  1510.2 15.9 convert_element_type.264
  1526.1 7.7 convolution_convert_fusion.6
  1535.3 9.8 convolution_convert_fusion.5
  1546.5 11.6 convolution_convert_fusion.4
  1558.2 13.4 multiply_bitcast_fusion
  1580.1 97.0 %reduce-scatter.12.cloned.1.call-done = bf16[64,16,768]{2,1,0:T(8,128)(2,1)} async-done(((bf16[64,256,768]{2,1,0:T(8,128)(2,1)}), bf16[64,16,768]{2,1,0:T(8,128)(2,1)}) %reduce-scatter.12.cloned.1.call-update) | async-done | bytes 1572880 | tf_op jit(solution)/shard_map/reduce_scatter | solution.py:260
  1677.1 246.5 %reduce-scatter.14.cloned.1.call-done = bf16[64,16,768]{2,1,0:T(8,128)(2,1)} async-done(((bf16[64,256,768]{2,1,0:T(8,128)(2,1)}), bf16[64,16,768]{2,1,0:T(8,128)(2,1)}) %reduce-scatter.14.cloned.1.call-update) | async-done | bytes 1572880 | tf_op jit(solution)/shard_map/reduce_scatter | solution.py:266
  1936.6 8.3 fusion.95
  1965.4 19.3 convolution_convert_fusion.1
  1988.7 56.4 %reduce-scatter.24.cloned.1.call-done = bf16[48,768]{1,0:T(8,128)(2,1)} async-done(((bf16[768,768]{1,0:T(8,128)(2,1)}), bf16[48,768]{1,0:T(8,128)(2,1)}) %reduce-scatter.24.cloned.1.call-update) | async-done | bytes 73744 | tf_op jit(solution)/shard_map/reduce_scatter | solution.py:312
  2045.1 70.9 %reduce-scatter.26.cloned.1.call-done = bf16[48,2304]{1,0:T(8,128)(2,1)} async-done(((bf16[768,2304]{1,0:T(8,128)(2,1)}), bf16[48,2304]{1,0:T(8,128)(2,1)}) %reduce-scatter.26.cloned.1.call-update) | async-done | bytes 221200 | tf_op jit(solution)/shard_map/reduce_scatter | solution.py:315
  2116.1 78.3 %reduce-scatter.30.cloned.1.call-done = bf16[48,3072]{1,0:T(8,128)(2,1)} async-done(((bf16[768,3072]{1,0:T(8,128)(2,1)}), bf16[48,3072]{1,0:T(8,128)(2,1)}) %reduce-scatter.30.cloned.1.call-update) | async-done | bytes 294928 | tf_op jit(solution)/shard_map/reduce_scatter | solution.py:321
  2194.3 78.7 %reduce-scatter.32.cloned.1.call-done = bf16[192,768]{1,0:T(8,128)(2,1)} async-done(((bf16[3072,768]{1,0:T(8,128)(2,1)}), bf16[192,768]{1,0:T(8,128)(2,1)}) %reduce-scatter.32.cloned.1.call-update) | async-done | bytes 294928 | tf_op jit(solution)/shard_map/reduce_scatter | solution.py:324
  2273.0 61.7 %reduce-scatter.18.cloned.1.call-done = bf16[48,768]{1,0:T(8,128)(2,1)} async-done(((bf16[768,768]{1,0:T(8,128)(2,1)}), bf16[48,768]{1,0:T(8,128)(2,1)}) %reduce-scatter.18.cloned.1.call-update) | async-done | bytes 73744 | tf_op jit(solution)/shard_map/reduce_scatter | solution.py:303
  2334.6 70.9 %reduce-scatter.22.cloned.1.call-done = bf16[48,2304]{1,0:T(8,128)(2,1)} async-done(((bf16[768,2304]{1,0:T(8,128)(2,1)}), bf16[48,2304]{1,0:T(8,128)(2,1)}) %reduce-scatter.22.cloned.1.call-update) | async-done | bytes 221200 | tf_op jit(solution)/shard_map/reduce_scatter | solution.py:309
  2405.5 123.6 %reduce-scatter.20.cloned.1.call-done = bf16[48,6912]{1,0:T(8,128)(2,1)} async-done(((bf16[768,6912]{1,0:T(8,128)(2,1)}), bf16[48,6912]{1,0:T(8,128)(2,1)}) %reduce-scatter.20.cloned.1.call-update) | async-done | bytes 663568 | tf_op jit(solution)/shard_map/reduce_scatter | solution.py:306
  2534.2 54.5 %reduce-scatter.16.cloned.1.call-done = bf16[16,768]{1,0:T(8,128)(2,1)} async-done(((bf16[256,768]{1,0:T(8,128)(2,1)}), bf16[16,768]{1,0:T(8,128)(2,1)}) %reduce-scatter.16.cloned.1.call-update) | async-done | bytes 24592 | tf_op jit(solution)/shard_map/reduce_scatter | solution.py:300
  2588.7 9.5 psum.63
  2599.6 50.0 %all-reduce.3.cloned.1.call-done = (bf16[48,768]{1,0:T(8,128)(2,1)}, bf16[48,6912]{1,0:T(8,128)(2,1)}, bf16[48,2304]{1,0:T(8,128)(2,1)}, bf16[48,768]{1,0:T(8,12...) async-done(((bf16[48,768]{1,0:T(8,128)(2,1)}, bf16[48,6912]{1,0:T(8,128)(2,1)}, ...) | async-done | bytes 1916944 | tf_op jit(solution)/shard_map/psum | solution.py:330
  (364 shorter events, 303.0 us)
Async XLA Ops:
  7.2 1130.3 %copy-start = (bf16[768,2304]{1,0:T(8,128)(2,1)S(1)}, bf16[768,2304]{1,0:T(8,128)(2,1)}, u32[]{:S(2)}) copy-start(bf16[768,2304]{1,0:T(8,128)(2,1)} %param.21) | copy-start | bytes 10616836
  7.2 1061.5 %all-gather.2.cloned.1.call-start = ((), (), s32[]{:S(2)}) async-start(), calls=%async_computation.11 | async-start | bytes 26738688 | tf_op jit(solution)/shard_map/all_gather | solution.py:134
  9.2 412.9 %copy-start.94 = (s32[64]{0:T(128)}, s32[64]{0:T(128)S(1)}, u32[]{:S(2)}) copy-start(s32[64]{0:T(128)S(1)} %convert_reduce_fusion.1) | copy-start | bytes 772
  62.5 1614.5 %reduce-scatter.12.cloned.1.call-start = ((), (), s32[]{:S(2)}) async-start(), calls=%async_computation.12 | async-start | bytes 26738688 | tf_op jit(solution)/shard_map/reduce_scatter | solution.py:260
  68.7 197.5 %copy-start.6 = (bf16[64,16,768]{2,1,0:T(8,128)(2,1)S(1)}, bf16[64,16,768]{2,1,0:T(8,128)(2,1)}, u32[]{:S(2)}) copy-start(bf16[64,16,768]{2,1,0:T(8,128)(2,1)} %reshape_squeeze.7) | copy-start | bytes 4718596
  68.7 57.5 %collective-permute-start = (bf16[64,16,768]{2,1,0:T(8,128)(2,1)}, bf16[64,16,768]{2,1,0:T(8,128)(2,1)S(1)}, u32[]{:S(2)}, u32[]{:S(2)}) collective-permute-start(bf16[64,16,768]{2,1,0:T(8,128)(2,1)} %reshape_squeeze.7), channel_id=1, source_target_pairs={{0,15},{1,0},{2,1},{3,2},{4,3},{5,4},{6,5},{7,6},{8,7},{9,8},{10,9... | collective-permute-start | bytes 4718600 | tf_op jit(solution)/shard_map/ppermute | solution.py:125
  126.2 284.7 %copy-start.14 = (bf16[64,16,768]{2,1,0:T(8,128)(2,1)}, bf16[64,16,768]{2,1,0:T(8,128)(2,1)S(1)}, u32[]{:S(2)}) copy-start(bf16[64,16,768]{2,1,0:T(8,128)(2,1)S(1)} %collective-permute-done) | copy-start | bytes 4718596
  128.6 137.5 %collective-permute-start.1 = (bf16[64,32,768]{2,1,0:T(8,128)(2,1)S(1)}, bf16[64,32,768]{2,1,0:T(8,128)(2,1)S(1)}, u32[]{:S(2)}, u32[]{:S(2)}) collective-permute-start(bf16[64,32,768]{2,1,0:T(8,128)(2,1)S(1)} %pad_maximum_fusion.2), channel_id=1, source_target_pairs={{0,14},{1,15},{2,0},{3,1},{4,2},{5,3},{6,4},{7,5},{8,6},{9,7},{10,... | collective-permute-start | bytes 9437192 | tf_op jit(solution)/shard_map/ppermute | solution.py:125
  266.2 144.8 %copy-start.11 = (bf16[64,32,768]{2,1,0:T(8,128)(2,1)}, bf16[64,32,768]{2,1,0:T(8,128)(2,1)S(1)}, u32[]{:S(2)}) copy-start(bf16[64,32,768]{2,1,0:T(8,128)(2,1)S(1)} %collective-permute-done.1) | copy-start | bytes 9437188
  266.9 144.0 %collective-permute-start.2 = (bf16[64,64,768]{2,1,0:T(8,128)(2,1)S(1)}, bf16[64,64,768]{2,1,0:T(8,128)(2,1)S(1)}, u32[]{:S(2)}, u32[]{:S(2)}) collective-permute-start(bf16[64,64,768]{2,1,0:T(8,128)(2,1)S(1)} %pad_maximum_fusion.1), channel_id=1, source_target_pairs={{0,12},{1,13},{2,14},{3,15},{4,0},{5,1},{6,2},{7,3},{8,4},{9,5},{1... | collective-permute-start | bytes 18874376 | tf_op jit(solution)/shard_map/ppermute | solution.py:125
  417.4 543.2 %collective-permute-start.3 = (bf16[64,128,768]{2,1,0:T(8,128)(2,1)}, bf16[64,128,768]{2,1,0:T(8,128)(2,1)}, u32[]{:S(2)}, u32[]{:S(2)}) collective-permute-start(bf16[64,128,768]{2,1,0:T(8,128)(2,1)} %pad_maximum_fusion), channel_id=1, source_target_pairs={{0,8},{1,9},{2,10},{3,11},{4,12},{5,13},{6,14},{7,15},{8,0},{9,1},... | collective-permute-start | bytes 37748744 | tf_op jit(solution)/shard_map/ppermute | solution.py:125
  419.2 9.6 slice-start.5
  431.9 539.6 %copy-start.7 = (bf16[64,16,768]{2,1,0:T(8,128)(2,1)S(1)}, bf16[64,16,768]{2,1,0:T(8,128)(2,1)}, u32[]{:S(2)}) copy-start(bf16[64,16,768]{2,1,0:T(8,128)(2,1)} %reshape_squeeze.7) | copy-start | bytes 4718596
  960.6 12.2 copy-start.15
  1059.2 8.6 copy-start.31
  1198.0 9.8 slice-start.7
  1215.2 27.9 %copy-start.25 = (f32[1024,768]{1,0:T(8,128)}, f32[1024,768]{1,0:T(8,128)S(1)}, u32[]{:S(2)}) copy-start(f32[1024,768]{1,0:T(8,128)S(1)} %fusion.86) | copy-start | bytes 9437188
  1280.6 12.6 slice-start
  1334.3 7.6 copy-start.79
  1334.3 7.6 copy-start.4
  1334.3 7.6 copy-start.35
  1334.3 7.6 copy-start.57
  1334.3 7.6 copy-start.72
  1334.3 10.5 copy-start.26
  1334.3 10.5 copy-start.27
  1334.3 10.5 copy-start.28
  1388.1 13.8 copy-start.5
  1434.8 488.8 %reduce-scatter.14.cloned.1.call-start = ((), (), s32[]{:S(2)}) async-start(), calls=%async_computation.13 | async-start | bytes 26738688 | tf_op jit(solution)/shard_map/reduce_scatter | solution.py:266
  1486.5 502.2 %reduce-scatter.28.cloned.1.call-start = ((), (), s32[]{:S(2)}) async-start(), calls=%async_computation.20 | async-start | bytes 1253376 | tf_op jit(solution)/shard_map/reduce_scatter | solution.py:318
  1502.2 542.9 %reduce-scatter.24.cloned.1.call-start = ((), (), s32[]{:S(2)}) async-start(), calls=%async_computation.18 | async-start | bytes 1253376 | tf_op jit(solution)/shard_map/reduce_scatter | solution.py:312
  1510.1 16.0 copy-start.47
  1510.1 605.9 %reduce-scatter.26.cloned.1.call-start = ((), (), s32[]{:S(2)}) async-start(), calls=%async_computation.19 | async-start | bytes 3760128 | tf_op jit(solution)/shard_map/reduce_scatter | solution.py:315
  1533.9 660.5 %reduce-scatter.30.cloned.1.call-start = ((), (), s32[]{:S(2)}) async-start(), calls=%async_computation.21 | async-start | bytes 5013504 | tf_op jit(solution)/shard_map/reduce_scatter | solution.py:321
  1545.1 727.9 %reduce-scatter.32.cloned.1.call-start = ((), (), s32[]{:S(2)}) async-start(), calls=%async_computation.22 | async-start | bytes 5013504 | tf_op jit(solution)/shard_map/reduce_scatter | solution.py:324
  1558.2 776.5 %reduce-scatter.18.cloned.1.call-start = ((), (), s32[]{:S(2)}) async-start(), calls=%async_computation.15 | async-start | bytes 1253376 | tf_op jit(solution)/shard_map/reduce_scatter | solution.py:303
  1926.1 10.5 slice-start.2
  1928.3 8.3 slice-start.3
  1928.3 8.3 slice-start.4
  1936.6 8.3 copy-start.74
  1936.6 8.3 copy-start.85
  1948.1 457.4 %reduce-scatter.22.cloned.1.call-start = ((), (), s32[]{:S(2)}) async-start(), calls=%async_computation.17 | async-start | bytes 3760128 | tf_op jit(solution)/shard_map/reduce_scatter | solution.py:309
  1965.4 563.8 %reduce-scatter.20.cloned.1.call-start = ((), (), s32[]{:S(2)}) async-start(), calls=%async_computation.16 | async-start | bytes 11280384 | tf_op jit(solution)/shard_map/reduce_scatter | solution.py:306
  1984.7 544.5 %copy-start.86 = (f32[64,16]{1,0:T(8,128)S(1)}, f32[64,16]{1,0:T(8,128)}, u32[]{:S(2)}) copy-start(f32[64,16]{1,0:T(8,128)} %get-tuple-element.14) | copy-start | bytes 12292
  1984.7 604.0 %reduce-scatter.16.cloned.1.call-start = ((), (), s32[]{:S(2)}) async-start(), calls=%async_computation.14 | async-start | bytes 417792 | tf_op jit(solution)/shard_map/reduce_scatter | solution.py:300
  1988.6 660.9 %all-reduce.3.cloned.1.call-start = ((), (), s32[]{:S(2)}) async-start(), calls=%async_computation.23 | async-start | bytes 3833856 | tf_op jit(solution)/shard_map/psum | solution.py:330
  2529.2 129.9 %copy-start.1 = (bf16[768,2304]{1,0:T(8,128)(2,1)S(1)}, bf16[768,2304]{1,0:T(8,128)(2,1)}, u32[]{:S(2)}) copy-start(bf16[768,2304]{1,0:T(8,128)(2,1)} %param.21) | copy-start | bytes 10616836
  2649.6 8.2 copy-start.88
  2649.6 8.9 copy-start.87
  (77 other events, 249.8 us)
Sparse Core Ops, SparseCore 0:
  62.7 221.0 all-gather.1
  1435.0 242.0 reduce-scatter.11
  1681.2 242.3 reduce-scatter.13
  1927.1 57.2 reduce-scatter.27
  1987.9 57.2 reduce-scatter.23
  2048.9 67.1 reduce-scatter.25
  2119.9 74.3 reduce-scatter.29
  2198.2 74.7 reduce-scatter.31
  2277.2 57.4 reduce-scatter.17
  2338.4 67.1 reduce-scatter.21
  2409.6 119.5 reduce-scatter.19
  2533.1 55.6 reduce-scatter.15
  2591.4 58.1 all-reduce.2
